TPU v7x, 32 devices: a whole 2x2x4 slice. The times are simulated.
32 devices in a mesh: fsdp: 8 (over z, x), ckpt: 4 (over y, core).
Axes of the slice: x: 2, y: 2, z: 4, core: 2. Of those that a mesh axis runs over, the one named last changes fastest.
Arguments:
- act_table: bfloat16 [4, 2048, 4096], P('ckpt', 'fsdp'), may hold values from -6 to 6
- token_ids: int32 [4, 2048], P('ckpt'), may hold values from 0 to 2047, each once within a row
- lengths: int32 [4, 8], P('ckpt'), may hold values from 1 to 384, 2048 in all within a row
- grads: bfloat16 [4, 2048, 14336], P('ckpt', 'fsdp'), may hold values from -0.19921875 to 0.19921875
- weights: bfloat16 [4, 8, 4096, 1792], P('ckpt', 'fsdp'), may hold values from -6 to 6
Outputs:
- merged: bfloat16 [8, 4096, 1792], P('fsdp', 'ckpt')
- merge_weight: float32 [8, 4096, 1792], P('fsdp', 'ckpt')
Inputs may be any that keep to these rules, and one draw needn't show every extreme that they name: `token_ids`: each checkpoint's row names every row of the activation table once. One checkpoint's lengths sum to 2048, and one of them is exactly 384.
All inputs are finite; a program needn't handle non-finite values.
Results may differ from a plain program's by a relative error of at most 0.001.
Values may be sent and summed in bfloat16 or wider, within the bound.
No kernel may reach another device: no remote copies, remote signals or barrier semaphores. Data moves between devices by JAX's collectives and lax.ppermute only.
A program may use at most 256 MiB of HBM per device.

v0:
```python
import jax
import jax.numpy as jnp
from jax import lax
from jax.sharding import PartitionSpec as P

NCB = 8
MOST = 384
prior_mass = 0.1


def example_fisher(act_rows, grad_rows, example_lengths, longest):
    row_starts = jnp.cumsum(example_lengths) - example_lengths
    padded_rows = jnp.concatenate(
        [act_rows, jnp.zeros((longest, act_rows.shape[1]), act_rows.dtype)], 0
    )
    padded_grads = jnp.concatenate(
        [grad_rows, jnp.zeros((longest, grad_rows.shape[1]), grad_rows.dtype)], 0
    )
    positions = jnp.arange(longest, dtype=jnp.int32)

    def add_example(example, running):
        row_start = row_starts[example]
        act_block = lax.dynamic_slice_in_dim(padded_rows, row_start, longest, 0)
        keep = (positions < example_lengths[example])[:, None]
        act_block = jnp.where(keep, act_block, jnp.zeros_like(act_block))
        grad_block = lax.dynamic_slice_in_dim(padded_grads, row_start, longest, 0)
        example_grad = lax.dot_general(
            act_block, grad_block, (((0,), (0,)), ((), ())), preferred_element_type=jnp.float32
        )
        return running + example_grad * example_grad

    start_value = jnp.zeros((act_rows.shape[1], grad_rows.shape[1]), jnp.float32)
    return lax.fori_loop(0, example_lengths.shape[0], add_example, start_value)


def body(act_table, token_ids, lengths, grads, weights):
    group_width = lax.axis_size("fsdp")
    row_blocks = group_width // NCB
    own_rows = act_table[0]
    local_count = own_rows.shape[0]
    feature_width = own_rows.shape[1] // row_blocks
    act_parts = jnp.broadcast_to(
        own_rows.reshape(local_count, row_blocks, 1, feature_width),
        (local_count, row_blocks, NCB, feature_width),
    )
    act_parts = act_parts.reshape(local_count, group_width * feature_width)
    table_rows = lax.all_to_all(act_parts, "fsdp", split_axis=1, concat_axis=0, tiled=True)
    act_rows = table_rows[token_ids[0]]
    own_grads = grads[0]
    grad_width = own_grads.shape[1]
    grad_parts = jnp.broadcast_to(
        own_grads.reshape(local_count, 1, grad_width), (local_count, row_blocks, grad_width)
    )
    grad_parts = grad_parts.reshape(local_count, row_blocks * grad_width)
    grad_rows = lax.all_to_all(grad_parts, "fsdp", split_axis=1, concat_axis=0, tiled=True)
    fisher = example_fisher(act_rows, grad_rows, lengths[0], MOST)
    fisher_mass = fisher + prior_mass
    own_weight = weights[0, 0]
    group_size = lax.axis_size("ckpt")
    weight_parts = lax.all_to_all(own_weight[None], "ckpt", split_axis=1, concat_axis=0, tiled=True)
    mass_parts = lax.all_to_all(fisher_mass[None], "ckpt", split_axis=1, concat_axis=0, tiled=True)
    numerator = jnp.sum(mass_parts * weight_parts.astype(jnp.float32), axis=0)
    denominator = jnp.sum(mass_parts, axis=0)
    return ((numerator / denominator).astype(jnp.bfloat16)[None], (denominator / group_size)[None])


def solution(mesh):
    placed = (
        P("ckpt", "fsdp", None),
        P("ckpt", None),
        P("ckpt", None),
        P("ckpt", "fsdp", None),
        P("ckpt", "fsdp", None, None),
    )
    return jax.shard_map(
        body,
        mesh=mesh,
        in_specs=placed,
        out_specs=(P("fsdp", "ckpt", None), P("fsdp", "ckpt", None)),
        check_vma=False,
    )
```

profile of v0, /device:TPU:0, one launch (start us, length us, event | category | flops | bytes accessed | tf_op | source)
XLA Modules:
  0.0 1270.1 jit_solution(4994978410783531105)
XLA Ops:
  0.6 8.2 copy.14
  8.9 4.6 copy.10
  13.5 167.8 %all_to_all.56 = bf16[256,8,1792]{2,0,1:T(8,128)(2,1)} all-to-all(bf16[256,8,1792]{2,0,1:T(8,128)(2,1)S(1)} %copy.10), channel_id=1, replica_groups=mesh['fsdp'=8,'ckpt'=4] {'fsdp'}, dimensions={1} | all-to-all | bytes 14680064 | tf_op jit(solution)/shard_map/all_to_all | solution.py:55
  181.3 6.0 broadcast_in_dim.40
  187.2 6.1 all-to-all-start
  193.5 26.1 %copy.16 = bf16[1,4096,1792]{2,0,1:T(2,128)(2,1)} copy(bf16[1,4096,1792]{2,1,0:T(8,128)(2,1)} %bitcast.41) | data formatting | bytes 29360128 | tf_op jit(solution)/shard_map/broadcast_in_dim;squeeze | solution.py:60
  220.1 147.2 %reduce = bf16[4096,1792]{1,0:T(8,128)(2,1)} reduce(bf16[4096,1,1792]{2,1,0:T(2,128)(2,1)} %bitcast.38, bf16[]{:T(256)} %broadcast.59), dimensions={1}, to_apply=%bitcast.30.reduce_sub_computation | reduce | bytes 29360130
  367.4 11.5 reshape.122
  378.9 7.0 concatenate.7
  385.9 169.2 %all-to-all-done = bf16[256,8,4096]{2,0,1:T(8,128)(2,1)} async-done(((bf16[256,8,4096]{2,0,1:T(8,128)(2,1)}), bf16[256,8,4096]{2,0,1:T(8,128)(2,1)}, u32[]{:S(2)}, u32[]{:S(2)}) %all-to-all-start) | async-done | bytes 16777248 | tf_op jit(solution)/shard_map/all_to_all | solution.py:47
  555.1 7.0 all-to-all-start.3
  562.1 36.6 %gather_fusion = bf16[2048,4096]{1,0:T(8,128)(2,1)} fusion(bf16[2048,4096]{1,0:T(8,128)(2,1)} %bitcast.5, s32[2048]{0:T(1024)S(1)} %broadcast_clamp_fusion), kind=kCustom, calls=%fused_computation | custom fusion | bytes 33562624 | tf_op jit(solution)/shard_map/gather | solution.py:48
  598.7 17.6 %concatenate.6 = bf16[2432,4096]{1,0:T(8,128)(2,1)} pad(bf16[2048,4096]{1,0:T(8,128)(2,1)} %gather_fusion, bf16[]{:T(256)} %constant.50.clone.1), padding=0_384x0_0 | pad | bytes 36700160 | tf_op jit(solution)/shard_map/concatenate | solution.py:13
  616.2 221.3 %while.14 = (s32[]{:T(128)}, f32[4096,1792]{1,0:T(8,128)}, s32[8]{0:T(128)S(1)}, s32[8]{0:T(128)S(1)}, bf16[2432,4096]{1,0:T(8,128)(2,1)}, /*index=5*/bf16[2432,1792]{1,0:T(8,128)(2,1)}, s32[]{:T(128)}, s32[]{:T(128)}, s32[]{:T(128)}) while((s32[]{:T(128)}, f32[4096,1792]{1,0:T(8,128)}, s32[8]{0:T(128)S(1)}, s32[8]{0:T(128)S(1)}, ...), condition=%wide.region_2.3_spmd.clone, body=%wide.region_1.2_spmd.clone.sunk | while | flops 5660738048 | bytes 63244708 | solution.py:33
  619.3 0.6 iota_compare_fusion.2
  620.0 15.1 %select_add_fusion.2 = f32[4096,1792]{1,0:T(8,128)} fusion(f32[4096,1792]{1,0:T(8,128)} %get-tuple-element.213, pred[]{:T(512)S(6)} %compare.5, bf16[2432,4096]{1,0:T(8,128)(2,1)} %get-tuple-element.225, s32[]{:T(128)S(6)} %select_n.41, pred[384]{0:T(512)(128)(4,1)S(1)} %iota_compare_fusion.2, bf16[2432,1792]{1,0:T(8,128)(2,1)} %get-tuple-element.226), kind=kOutput, calls=%fused_computation.2.clone.1 | convolution fusion | flops 5660737536 | bytes 63244160 | tf_op jit(solution)/shard_map/while/body/eval_jaxpr/dot_general | solution.py:27
  638.9 25.1 %select_add_fusion.2 = f32[4096,1792]{1,0:T(8,128)} fusion(f32[4096,1792]{1,0:T(8,128)} %get-tuple-element.213, pred[]{:T(512)S(6)} %compare.5, bf16[2432,4096]{1,0:T(8,128)(2,1)} %get-tuple-element.225, s32[]{:T(128)S(6)} %select_n.41, pred[384]{0:T(512)(128)(4,1)S(1)} %iota_compare_fusion.2, bf16[2432,1792]{1,0:T(8,128)(2,1)} %get-tuple-element.226), kind=kOutput, calls=%fused_computation.2.clone.1 | convolution fusion | flops 5660737536 | bytes 63244160 | tf_op jit(solution)/shard_map/while/body/eval_jaxpr/dot_general | solution.py:27
  667.8 25.1 %select_add_fusion.2 = f32[4096,1792]{1,0:T(8,128)} fusion(f32[4096,1792]{1,0:T(8,128)} %get-tuple-element.213, pred[]{:T(512)S(6)} %compare.5, bf16[2432,4096]{1,0:T(8,128)(2,1)} %get-tuple-element.225, s32[]{:T(128)S(6)} %select_n.41, pred[384]{0:T(512)(128)(4,1)S(1)} %iota_compare_fusion.2, bf16[2432,1792]{1,0:T(8,128)(2,1)} %get-tuple-element.226), kind=kOutput, calls=%fused_computation.2.clone.1 | convolution fusion | flops 5660737536 | bytes 63244160 | tf_op jit(solution)/shard_map/while/body/eval_jaxpr/dot_general | solution.py:27
  696.7 25.1 %select_add_fusion.2 = f32[4096,1792]{1,0:T(8,128)} fusion(f32[4096,1792]{1,0:T(8,128)} %get-tuple-element.213, pred[]{:T(512)S(6)} %compare.5, bf16[2432,4096]{1,0:T(8,128)(2,1)} %get-tuple-element.225, s32[]{:T(128)S(6)} %select_n.41, pred[384]{0:T(512)(128)(4,1)S(1)} %iota_compare_fusion.2, bf16[2432,1792]{1,0:T(8,128)(2,1)} %get-tuple-element.226), kind=kOutput, calls=%fused_computation.2.clone.1 | convolution fusion | flops 5660737536 | bytes 63244160 | tf_op jit(solution)/shard_map/while/body/eval_jaxpr/dot_general | solution.py:27
  725.6 25.1 %select_add_fusion.2 = f32[4096,1792]{1,0:T(8,128)} fusion(f32[4096,1792]{1,0:T(8,128)} %get-tuple-element.213, pred[]{:T(512)S(6)} %compare.5, bf16[2432,4096]{1,0:T(8,128)(2,1)} %get-tuple-element.225, s32[]{:T(128)S(6)} %select_n.41, pred[384]{0:T(512)(128)(4,1)S(1)} %iota_compare_fusion.2, bf16[2432,1792]{1,0:T(8,128)(2,1)} %get-tuple-element.226), kind=kOutput, calls=%fused_computation.2.clone.1 | convolution fusion | flops 5660737536 | bytes 63244160 | tf_op jit(solution)/shard_map/while/body/eval_jaxpr/dot_general | solution.py:27
  754.5 25.1 %select_add_fusion.2 = f32[4096,1792]{1,0:T(8,128)} fusion(f32[4096,1792]{1,0:T(8,128)} %get-tuple-element.213, pred[]{:T(512)S(6)} %compare.5, bf16[2432,4096]{1,0:T(8,128)(2,1)} %get-tuple-element.225, s32[]{:T(128)S(6)} %select_n.41, pred[384]{0:T(512)(128)(4,1)S(1)} %iota_compare_fusion.2, bf16[2432,1792]{1,0:T(8,128)(2,1)} %get-tuple-element.226), kind=kOutput, calls=%fused_computation.2.clone.1 | convolution fusion | flops 5660737536 | bytes 63244160 | tf_op jit(solution)/shard_map/while/body/eval_jaxpr/dot_general | solution.py:27
  783.4 25.2 %select_add_fusion.2 = f32[4096,1792]{1,0:T(8,128)} fusion(f32[4096,1792]{1,0:T(8,128)} %get-tuple-element.213, pred[]{:T(512)S(6)} %compare.5, bf16[2432,4096]{1,0:T(8,128)(2,1)} %get-tuple-element.225, s32[]{:T(128)S(6)} %select_n.41, pred[384]{0:T(512)(128)(4,1)S(1)} %iota_compare_fusion.2, bf16[2432,1792]{1,0:T(8,128)(2,1)} %get-tuple-element.226), kind=kOutput, calls=%fused_computation.2.clone.1 | convolution fusion | flops 5660737536 | bytes 63244160 | tf_op jit(solution)/shard_map/while/body/eval_jaxpr/dot_general | solution.py:27
  812.4 25.1 %select_add_fusion.2 = f32[4096,1792]{1,0:T(8,128)} fusion(f32[4096,1792]{1,0:T(8,128)} %get-tuple-element.213, pred[]{:T(512)S(6)} %compare.5, bf16[2432,4096]{1,0:T(8,128)(2,1)} %get-tuple-element.225, s32[]{:T(128)S(6)} %select_n.41, pred[384]{0:T(512)(128)(4,1)S(1)} %iota_compare_fusion.2, bf16[2432,1792]{1,0:T(8,128)(2,1)} %get-tuple-element.226), kind=kOutput, calls=%fused_computation.2.clone.1 | convolution fusion | flops 5660737536 | bytes 63244160 | tf_op jit(solution)/shard_map/while/body/eval_jaxpr/dot_general | solution.py:27
  837.5 21.6 %broadcast_add_fusion = f32[4096,1792]{1,0:T(8,128)} fusion(f32[4096,1792]{1,0:T(8,128)} %get-tuple-element.126), kind=kLoop, calls=%fused_computation.12 | loop fusion | flops 7340032 | bytes 58720256 | tf_op jit(solution)/shard_map/add | solution.py:57
  859.1 24.0 %broadcast_in_dim.41 = f32[1,4096,1792]{2,0,1:T(1,128)} reshape(f32[4096,1792]{1,0:T(8,128)} %broadcast_add_fusion) | data formatting | bytes 58720256 | tf_op jit(solution)/shard_map/broadcast_in_dim | solution.py:61
  883.0 9.4 all-to-all-start.2
  892.4 32.2 %reshape.123 = bf16[4096,1,1792]{2,1,0:T(2,128)(2,1)} reshape(bf16[4,2,917504]{2,1,0:T(2,128)(2,1)} %all-to-all-done.3) | data formatting | bytes 29360128
  924.7 23.8 %copy.13 = f32[1,4096,1792]{2,1,0:T(8,128)} copy(bf16[1,4096,1792]{2,0,1:T(2,128)(2,1)} %bitcast.37) | data formatting | bytes 44040192
  948.5 261.5 %all-to-all-done.2 = f32[1,4096,1792]{2,0,1:T(1,128)} async-done(((f32[1,4096,1792]{2,0,1:T(1,128)}), f32[1,4096,1792]{2,0,1:T(1,128)}, u32[]{:S(2)}, u32[]{:S(2)}) %all-to-all-start.2) | async-done | bytes 29360160 | tf_op jit(solution)/shard_map/all_to_all | solution.py:61
  1210.0 23.9 %copy.12 = f32[1,4096,1792]{2,1,0:T(8,128)} copy(f32[1,4096,1792]{2,0,1:T(1,128)} %all-to-all-done.2) | data formatting | bytes 58720256
  1233.9 25.5 %fusion.10 = (f32[1024,1792]{1,0:T(8,128)}, f32[1024,1792]{1,0:T(8,128)}) fusion(f32[4,1024,1792]{2,1,0:T(8,128)} %bitcast.36, f32[4,1024,1792]{2,1,0:T(8,128)} %bitcast.35), kind=kLoop, calls=%fused_computation.19 | loop fusion | flops 18350080 | bytes 73400320 | tf_op jit(solution)/shard_map/reduce_sum | solution.py:63
  1259.4 10.7 multiply_bitcast_fusion
  (36 shorter events, 14.6 us)
Async XLA Ops:
  8.9 172.4 %copy-start = (bf16[1,256,4096]{2,1,0:T(8,128)(2,1)S(1)}, bf16[1,256,4096]{2,1,0:T(8,128)(2,1)}, u32[]{:S(2)}) copy-start(bf16[1,256,4096]{2,1,0:T(8,128)(2,1)} %param.7) | copy-start | bytes 6291460
  187.2 6.1 copy-start.2
  187.2 367.8 %all-to-all-start = ((bf16[256,8,4096]{2,0,1:T(8,128)(2,1)}), bf16[256,8,4096]{2,0,1:T(8,128)(2,1)}, u32[]{:S(2)}, u32[]{:S(2)}) async-start(bf16[256,8,4096]{2,0,1:T(8,128)(2,1)} %broadcast_in_dim.40), calls=%async_computation | async-start | bytes 33554432 | tf_op jit(solution)/shard_map/all_to_all | solution.py:47
  367.4 11.5 copy-start.1
  555.1 328.0 %all-to-all-start.3 = ((bf16[4,2,917504]{2,1,0:T(2,128)(2,1)}), bf16[4,2,917504]{2,1,0:T(2,128)(2,1)}, u32[]{:S(2)}, u32[]{:S(2)}) async-start(bf16[4,2,917504]{2,1,0:T(2,128)(2,1)} %reshape.122), calls=%async_computation.3 | async-start | bytes 29360128 | tf_op jit(solution)/shard_map/all_to_all | solution.py:60
  883.0 327.0 %all-to-all-start.2 = ((f32[1,4096,1792]{2,0,1:T(1,128)}), f32[1,4096,1792]{2,0,1:T(1,128)}, u32[]{:S(2)}, u32[]{:S(2)}) async-start(f32[1,4096,1792]{2,0,1:T(1,128)} %broadcast_in_dim.41), calls=%async_computation.2 | async-start | bytes 58720256 | tf_op jit(solution)/shard_map/all_to_all | solution.py:61
where the time goes:
time: 1270 us
  waiting for transfers between devices  431 us (34%)
  local copies, waits for them, and re-layouts  231 us (18%)
  other arithmetic  210 us (17%)
  matrix products  191 us (15%)
  blocking collectives  168 us (13%)
  starting transfers between devices  22.5 us (2%)
  loops' own time  15.7 us (1%)
    all_to_all x1, waiting for transfers between devices, body(): lax.all_to_all(fisher_mass[None], 'ckpt', split_axis=1, concat_axis=0, ti...  262 us
    dot_general x8, matrix products, add_example(): lax.dot_general(act_block, grad_block, (((0,), (0,)), ((), ())), preferre...  191 us
    all_to_all x1, waiting for transfers between devices, body(): lax.all_to_all(act_parts, 'fsdp', split_axis=1, concat_axis=0, tiled=True)  169 us
    all_to_all x1, blocking collectives, body(): lax.all_to_all(grad_parts, 'fsdp', split_axis=1, concat_axis=0, tiled=True)  168 us
    unnamed x2, other arithmetic  147 us
    unnamed x12, local copies, waits for them, and re-layouts  100 us
    gather x1, local copies, waits for them, and re-layouts, body(): act_rows = table_rows[token_ids[0]]  36.6 us
    another operation x1, local copies, waits for them, and re-layouts, body(): own_weight[None]  26.1 us
  transfers between devices with their start and end apart: 3, of which 2 were waited for; matrix products, arithmetic and copies ran while one was open for 44% of the time, Pallas kernels for 0%

commit v1 on v0

--- a/solution.py
+++ b/solution.py
@@ -6,6 +6,29 @@
 NCB = 8
 MOST = 384
 prior_mass = 0.1
+
+
+def split_up(shard, dim, devices):
+    before, after = (shard.shape[:dim], shard.shape[dim + 1 :])
+    return jnp.moveaxis(shard.reshape(*before, devices, -1, *after), dim, 0)
+
+
+def laid_out(blocks, dim):
+    blocks = jnp.moveaxis(blocks, 0, dim)
+    shape = blocks.shape
+    return blocks.reshape(*shape[:dim], shape[dim] * shape[dim + 1], *shape[dim + 2 :])
+
+
+def sent_to_each(x, axis, split_dim, concat_dim):
+    devices, index = (lax.axis_size(axis), lax.axis_index(axis))
+    tiles = split_up(x, split_dim, devices)
+    whole = tiles
+    for step in range(1, devices):
+        target, source = ((index + step) % devices, (index - step) % devices)
+        sent = lax.dynamic_index_in_dim(tiles, target, 0)
+        theirs = lax.ppermute(sent, axis, [(i, (i + step) % devices) for i in range(devices)])
+        whole = lax.dynamic_update_slice_in_dim(whole, theirs, source, axis=0)
+    return laid_out(whole, concat_dim)
 
 
 def example_fisher(act_rows, grad_rows, example_lengths, longest):
@@ -44,7 +67,7 @@
         (local_count, row_blocks, NCB, feature_width),
     )
     act_parts = act_parts.reshape(local_count, group_width * feature_width)
-    table_rows = lax.all_to_all(act_parts, "fsdp", split_axis=1, concat_axis=0, tiled=True)
+    table_rows = sent_to_each(act_parts, "fsdp", 1, 0)
     act_rows = table_rows[token_ids[0]]
     own_grads = grads[0]
     grad_width = own_grads.shape[1]

time: 1270 us -> 1270 us (level)
  the two profiles are of different devices: /device:TPU:0 before, /device:TPU:26 now
where the time goes in v1:
time: 1270 us; the launch traced here: 1260 us
  waiting for transfers between devices  565 us (44%)
  local copies, waits for them, and re-layouts  247 us (19%)
  other arithmetic  210 us (17%)
  matrix products  191 us (15%)
  starting transfers between devices  35.4 us (3%)
  loops' own time  15.7 us (1%)
    ppermute x7, waiting for transfers between devices, sent_to_each(): lax.ppermute(sent, axis, [(i, (i + step) % devices) for i in range(device...  304 us
    all_to_all x1, waiting for transfers between devices, body(): lax.all_to_all(fisher_mass[None], 'ckpt', split_axis=1, concat_axis=0, ti...  262 us
    dot_general x8, matrix products, add_example(): lax.dot_general(act_block, grad_block, (((0,), (0,)), ((), ())), preferre...  191 us
    unnamed x2, other arithmetic  147 us
    unnamed x12, local copies, waits for them, and re-layouts  97.1 us
    gather x1, local copies, waits for them, and re-layouts, body(): act_rows = table_rows[token_ids[0]]  36.5 us
    another operation x1, local copies, waits for them, and re-layouts, body(): own_weight[None]  26.1 us
    reduce_sum x1, other arithmetic, body(): denominator = jnp.sum(mass_parts, axis=0)  25.5 us
  transfers between devices with their start and end apart: 10, of which 4 were waited for; matrix products, arithmetic and copies ran while one was open for 46% of the time, Pallas kernels for 0%

profile of v1, /device:TPU:26, one launch (start us, length us, event | category | flops | bytes accessed | tf_op | source)
XLA Modules:
  0.0 1265.0 jit_solution(4095054187995246616)
XLA Ops:
  0.6 5.2 copy.14
  10.3 6.0 all-to-all-start
  23.1 26.1 %copy.16 = bf16[1,4096,1792]{2,0,1:T(2,128)(2,1)} copy(bf16[1,4096,1792]{2,1,0:T(8,128)(2,1)} %bitcast.38) | data formatting | bytes 29360128 | tf_op jit(solution)/shard_map/broadcast_in_dim;squeeze | solution.py:83
  49.7 147.2 %reduce = bf16[4096,1792]{1,0:T(8,128)(2,1)} reduce(bf16[4096,1,1792]{2,1,0:T(2,128)(2,1)} %bitcast.36, bf16[]{:T(256)} %broadcast.74), dimensions={1}, to_apply=%bitcast.28.reduce_sub_computation | reduce | bytes 29360130
  196.8 11.5 reshape.134
  209.8 6.0 transpose.12
  219.0 6.6 collective-permute-done.1
  225.6 5.4 collective-permute-start.6
  234.1 36.5 %collective-permute-done.2 = bf16[1,256,4096]{2,1,0:T(8,128)(2,1)} collective-permute-done((bf16[1,256,4096]{2,1,0:T(8,128)(2,1)S(1)}, bf16[1,256,4096]{2,1,0:T(8,128)(2,1)}, u32[]{:S(2)}, u32[]{:S(2)}) %collective-permute-start.2) | collective-permute-done | bytes 2097184 | tf_op jit(solution)/shard_map/ppermute | solution.py:29
  273.7 260.5 %collective-permute-done.3 = bf16[1,256,4096]{2,1,0:T(8,128)(2,1)} collective-permute-done((bf16[1,256,4096]{2,1,0:T(8,128)(2,1)S(1)}, bf16[1,256,4096]{2,1,0:T(8,128)(2,1)}, u32[]{:S(2)}, u32[]{:S(2)}) %collective-permute-start.3) | collective-permute-done | bytes 2097184 | tf_op jit(solution)/shard_map/ppermute | solution.py:29
  543.4 36.5 %gather_fusion = bf16[2048,4096]{1,0:T(8,128)(2,1)} fusion(bf16[2048,4096]{1,0:T(8,128)(2,1)} %bitcast.4, s32[2048]{0:T(1024)S(1)} %broadcast_clamp_fusion), kind=kCustom, calls=%fused_computation | custom fusion | bytes 33562624 | tf_op jit(solution)/shard_map/gather | solution.py:71
  580.0 17.5 %concatenate.6 = bf16[2432,4096]{1,0:T(8,128)(2,1)} pad(bf16[2048,4096]{1,0:T(8,128)(2,1)} %gather_fusion, bf16[]{:T(256)} %constant.143.clone.1), padding=0_384x0_0 | pad | bytes 36700160 | tf_op jit(solution)/shard_map/concatenate | solution.py:36
  597.5 6.7 all-to-all-start.2
  604.2 7.1 concatenate.7
  611.3 220.9 %while.14 = (s32[]{:T(128)}, f32[4096,1792]{1,0:T(8,128)}, s32[8]{0:T(128)S(1)}, s32[8]{0:T(128)S(1)}, bf16[2432,4096]{1,0:T(8,128)(2,1)}, /*index=5*/bf16[2432,1792]{1,0:T(8,128)(2,1)}, s32[]{:T(128)}, s32[]{:T(128)}, s32[]{:T(128)}) while((s32[]{:T(128)}, f32[4096,1792]{1,0:T(8,128)}, s32[8]{0:T(128)S(1)}, s32[8]{0:T(128)S(1)}, ...), condition=%wide.region_2.3_spmd.clone, body=%wide.region_1.2_spmd.clone.sunk | while | flops 5660738048 | bytes 63244708 | solution.py:56
  615.1 15.1 %select_add_fusion.2 = f32[4096,1792]{1,0:T(8,128)} fusion(f32[4096,1792]{1,0:T(8,128)} %get-tuple-element.213, pred[]{:T(512)S(6)} %compare.12, bf16[2432,4096]{1,0:T(8,128)(2,1)} %get-tuple-element.225, s32[]{:T(128)S(6)} %select_n.129, pred[384]{0:T(512)(128)(4,1)S(1)} %iota_compare_fusion.2, bf16[2432,1792]{1,0:T(8,128)(2,1)} %get-tuple-element.226), kind=kOutput, calls=%fused_computation.2.clone.1 | convolution fusion | flops 5660737536 | bytes 63244160 | tf_op jit(solution)/shard_map/while/body/eval_jaxpr/dot_general | solution.py:50
  633.9 25.1 %select_add_fusion.2 = f32[4096,1792]{1,0:T(8,128)} fusion(f32[4096,1792]{1,0:T(8,128)} %get-tuple-element.213, pred[]{:T(512)S(6)} %compare.12, bf16[2432,4096]{1,0:T(8,128)(2,1)} %get-tuple-element.225, s32[]{:T(128)S(6)} %select_n.129, pred[384]{0:T(512)(128)(4,1)S(1)} %iota_compare_fusion.2, bf16[2432,1792]{1,0:T(8,128)(2,1)} %get-tuple-element.226), kind=kOutput, calls=%fused_computation.2.clone.1 | convolution fusion | flops 5660737536 | bytes 63244160 | tf_op jit(solution)/shard_map/while/body/eval_jaxpr/dot_general | solution.py:50
  662.8 25.1 %select_add_fusion.2 = f32[4096,1792]{1,0:T(8,128)} fusion(f32[4096,1792]{1,0:T(8,128)} %get-tuple-element.213, pred[]{:T(512)S(6)} %compare.12, bf16[2432,4096]{1,0:T(8,128)(2,1)} %get-tuple-element.225, s32[]{:T(128)S(6)} %select_n.129, pred[384]{0:T(512)(128)(4,1)S(1)} %iota_compare_fusion.2, bf16[2432,1792]{1,0:T(8,128)(2,1)} %get-tuple-element.226), kind=kOutput, calls=%fused_computation.2.clone.1 | convolution fusion | flops 5660737536 | bytes 63244160 | tf_op jit(solution)/shard_map/while/body/eval_jaxpr/dot_general | solution.py:50
  691.7 25.1 %select_add_fusion.2 = f32[4096,1792]{1,0:T(8,128)} fusion(f32[4096,1792]{1,0:T(8,128)} %get-tuple-element.213, pred[]{:T(512)S(6)} %compare.12, bf16[2432,4096]{1,0:T(8,128)(2,1)} %get-tuple-element.225, s32[]{:T(128)S(6)} %select_n.129, pred[384]{0:T(512)(128)(4,1)S(1)} %iota_compare_fusion.2, bf16[2432,1792]{1,0:T(8,128)(2,1)} %get-tuple-element.226), kind=kOutput, calls=%fused_computation.2.clone.1 | convolution fusion | flops 5660737536 | bytes 63244160 | tf_op jit(solution)/shard_map/while/body/eval_jaxpr/dot_general | solution.py:50
  720.5 25.1 %select_add_fusion.2 = f32[4096,1792]{1,0:T(8,128)} fusion(f32[4096,1792]{1,0:T(8,128)} %get-tuple-element.213, pred[]{:T(512)S(6)} %compare.12, bf16[2432,4096]{1,0:T(8,128)(2,1)} %get-tuple-element.225, s32[]{:T(128)S(6)} %select_n.129, pred[384]{0:T(512)(128)(4,1)S(1)} %iota_compare_fusion.2, bf16[2432,1792]{1,0:T(8,128)(2,1)} %get-tuple-element.226), kind=kOutput, calls=%fused_computation.2.clone.1 | convolution fusion | flops 5660737536 | bytes 63244160 | tf_op jit(solution)/shard_map/while/body/eval_jaxpr/dot_general | solution.py:50
  749.4 25.1 %select_add_fusion.2 = f32[4096,1792]{1,0:T(8,128)} fusion(f32[4096,1792]{1,0:T(8,128)} %get-tuple-element.213, pred[]{:T(512)S(6)} %compare.12, bf16[2432,4096]{1,0:T(8,128)(2,1)} %get-tuple-element.225, s32[]{:T(128)S(6)} %select_n.129, pred[384]{0:T(512)(128)(4,1)S(1)} %iota_compare_fusion.2, bf16[2432,1792]{1,0:T(8,128)(2,1)} %get-tuple-element.226), kind=kOutput, calls=%fused_computation.2.clone.1 | convolution fusion | flops 5660737536 | bytes 63244160 | tf_op jit(solution)/shard_map/while/body/eval_jaxpr/dot_general | solution.py:50
  778.2 25.1 %select_add_fusion.2 = f32[4096,1792]{1,0:T(8,128)} fusion(f32[4096,1792]{1,0:T(8,128)} %get-tuple-element.213, pred[]{:T(512)S(6)} %compare.12, bf16[2432,4096]{1,0:T(8,128)(2,1)} %get-tuple-element.225, s32[]{:T(128)S(6)} %select_n.129, pred[384]{0:T(512)(128)(4,1)S(1)} %iota_compare_fusion.2, bf16[2432,1792]{1,0:T(8,128)(2,1)} %get-tuple-element.226), kind=kOutput, calls=%fused_computation.2.clone.1 | convolution fusion | flops 5660737536 | bytes 63244160 | tf_op jit(solution)/shard_map/while/body/eval_jaxpr/dot_general | solution.py:50
  807.1 25.1 %select_add_fusion.2 = f32[4096,1792]{1,0:T(8,128)} fusion(f32[4096,1792]{1,0:T(8,128)} %get-tuple-element.213, pred[]{:T(512)S(6)} %compare.12, bf16[2432,4096]{1,0:T(8,128)(2,1)} %get-tuple-element.225, s32[]{:T(128)S(6)} %select_n.129, pred[384]{0:T(512)(128)(4,1)S(1)} %iota_compare_fusion.2, bf16[2432,1792]{1,0:T(8,128)(2,1)} %get-tuple-element.226), kind=kOutput, calls=%fused_computation.2.clone.1 | convolution fusion | flops 5660737536 | bytes 63244160 | tf_op jit(solution)/shard_map/while/body/eval_jaxpr/dot_general | solution.py:50
  832.2 21.7 %broadcast_add_fusion = f32[4096,1792]{1,0:T(8,128)} fusion(f32[4096,1792]{1,0:T(8,128)} %get-tuple-element.126), kind=kLoop, calls=%fused_computation.12 | loop fusion | flops 7340032 | bytes 58720256 | tf_op jit(solution)/shard_map/add | solution.py:80
  853.9 24.0 %broadcast_in_dim.38 = f32[1,4096,1792]{2,0,1:T(1,128)} reshape(f32[4096,1792]{1,0:T(8,128)} %broadcast_add_fusion) | data formatting | bytes 58720256 | tf_op jit(solution)/shard_map/broadcast_in_dim | solution.py:84
  877.8 9.4 all-to-all-start.1
  887.3 32.2 %reshape.135 = bf16[4096,1,1792]{2,1,0:T(2,128)(2,1)} reshape(bf16[4,2,917504]{2,1,0:T(2,128)(2,1)} %all-to-all-done.2) | data formatting | bytes 29360128
  919.4 23.8 %copy.13 = f32[1,4096,1792]{2,1,0:T(8,128)} copy(bf16[1,4096,1792]{2,0,1:T(2,128)(2,1)} %bitcast.35) | data formatting | bytes 44040192
  943.3 261.7 %all-to-all-done.1 = f32[1,4096,1792]{2,0,1:T(1,128)} async-done(((f32[1,4096,1792]{2,0,1:T(1,128)}), f32[1,4096,1792]{2,0,1:T(1,128)}, u32[]{:S(2)}, u32[]{:S(2)}) %all-to-all-start.1) | async-done | bytes 29360160 | tf_op jit(solution)/shard_map/all_to_all | solution.py:84
  1205.0 23.8 %copy.12 = f32[1,4096,1792]{2,1,0:T(8,128)} copy(f32[1,4096,1792]{2,0,1:T(1,128)} %all-to-all-done.1) | data formatting | bytes 58720256
  1228.8 25.5 %fusion.10 = (f32[1024,1792]{1,0:T(8,128)}, f32[1024,1792]{1,0:T(8,128)}) fusion(f32[4,1024,1792]{2,1,0:T(8,128)} %bitcast.34, f32[4,1024,1792]{2,1,0:T(8,128)} %bitcast.33), kind=kLoop, calls=%fused_computation.26 | loop fusion | flops 18350080 | bytes 73400320 | tf_op jit(solution)/shard_map/reduce_sum | solution.py:86
  1254.3 10.7 multiply_bitcast_fusion
  (56 shorter events, 46.3 us)
Async XLA Ops:
  5.8 10.5 copy-start
  5.8 16.9 %copy-start.1 = (s32[1,2048]{1,0:T(1,128)S(1)}, s32[1,2048]{1,0:T(1,128)}, u32[]{:S(2)}) copy-start(s32[1,2048]{1,0:T(1,128)} %param.8) | copy-start | bytes 24580
  5.8 16.9 %copy-start.2 = (s32[1,8]{1,0:T(1,128)S(1)}, s32[1,8]{1,0:T(1,128)}, u32[]{:S(2)}) copy-start(s32[1,8]{1,0:T(1,128)} %param.9) | copy-start | bytes 100
  10.3 587.2 %all-to-all-start = ((bf16[256,8,1792]{2,0,1:T(8,128)(2,1)}), bf16[256,8,1792]{2,0,1:T(8,128)(2,1)}, u32[]{:S(2)}, u32[]{:S(2)}) async-start(bf16[256,8,1792]{2,0,1:T(8,128)(2,1)} %copy.10), calls=%async_computation | async-start | bytes 14680064 | tf_op jit(solution)/shard_map/all_to_all | solution.py:78
  16.3 192.1 %collective-permute-start = (bf16[1,256,4096]{2,1,0:T(8,128)(2,1)S(1)}, bf16[1,256,4096]{2,1,0:T(8,128)(2,1)}, u32[]{:S(2)}, u32[]{:S(2)}) collective-permute-start(bf16[1,256,4096]{2,1,0:T(8,128)(2,1)S(1)} %copy-done), channel_id=1, source_target_pairs={{0,4},{4,8},{8,12},{12,16},{16,20},{20,24},{24,28},{28,0},{1,5},{5... | collective-permute-start | bytes 6291464 | tf_op jit(solution)/shard_map/ppermute | solution.py:29
  16.3 209.2 %collective-permute-start.1 = (bf16[1,256,4096]{2,1,0:T(8,128)(2,1)S(1)}, bf16[1,256,4096]{2,1,0:T(8,128)(2,1)}, u32[]{:S(2)}, u32[]{:S(2)}) collective-permute-start(bf16[1,256,4096]{2,1,0:T(8,128)(2,1)S(1)} %copy-done), channel_id=1, source_target_pairs={{0,8},{4,12},{8,16},{12,20},{16,24},{20,28},{24,0},{28,4},{1,9},{5... | collective-permute-start | bytes 6291464 | tf_op jit(solution)/shard_map/ppermute | solution.py:29
  18.3 252.2 %collective-permute-start.2 = (bf16[1,256,4096]{2,1,0:T(8,128)(2,1)S(1)}, bf16[1,256,4096]{2,1,0:T(8,128)(2,1)}, u32[]{:S(2)}, u32[]{:S(2)}) collective-permute-start(bf16[1,256,4096]{2,1,0:T(8,128)(2,1)S(1)} %copy-done), channel_id=1, source_target_pairs={{0,12},{4,16},{8,20},{12,24},{16,28},{20,0},{24,4},{28,8},{1,13},{... | collective-permute-start | bytes 6291464 | tf_op jit(solution)/shard_map/ppermute | solution.py:29
  19.8 514.4 %collective-permute-start.3 = (bf16[1,256,4096]{2,1,0:T(8,128)(2,1)S(1)}, bf16[1,256,4096]{2,1,0:T(8,128)(2,1)}, u32[]{:S(2)}, u32[]{:S(2)}) collective-permute-start(bf16[1,256,4096]{2,1,0:T(8,128)(2,1)S(1)} %copy-done), channel_id=1, source_target_pairs={{0,16},{4,20},{8,24},{12,28},{16,0},{20,4},{24,8},{28,12},{1,17},{... | collective-permute-start | bytes 6291464 | tf_op jit(solution)/shard_map/ppermute | solution.py:29
  21.2 516.1 %collective-permute-start.4 = (bf16[1,256,4096]{2,1,0:T(8,128)(2,1)S(1)}, bf16[1,256,4096]{2,1,0:T(8,128)(2,1)}, u32[]{:S(2)}, u32[]{:S(2)}) collective-permute-start(bf16[1,256,4096]{2,1,0:T(8,128)(2,1)S(1)} %copy-done), channel_id=1, source_target_pairs={{0,20},{4,24},{8,28},{12,0},{16,4},{20,8},{24,12},{28,16},{1,21},{... | collective-permute-start | bytes 6291464 | tf_op jit(solution)/shard_map/ppermute | solution.py:29
  208.3 332.2 %collective-permute-start.5 = (bf16[1,256,4096]{2,1,0:T(8,128)(2,1)S(1)}, bf16[1,256,4096]{2,1,0:T(8,128)(2,1)S(1)}, u32[]{:S(2)}, u32[]{:S(2)}) collective-permute-start(bf16[1,256,4096]{2,1,0:T(8,128)(2,1)S(1)} %copy-done), channel_id=1, source_target_pairs={{0,24},{4,28},{8,0},{12,4},{16,8},{20,12},{24,16},{28,20},{1,25},{... | collective-permute-start | bytes 6291464 | tf_op jit(solution)/shard_map/ppermute | solution.py:29
  225.6 316.4 %collective-permute-start.6 = (bf16[1,256,4096]{2,1,0:T(8,128)(2,1)S(1)}, bf16[1,256,4096]{2,1,0:T(8,128)(2,1)S(1)}, u32[]{:S(2)}, u32[]{:S(2)}) collective-permute-start(bf16[1,256,4096]{2,1,0:T(8,128)(2,1)S(1)} %copy-done), channel_id=1, source_target_pairs={{0,28},{4,0},{8,4},{12,8},{16,12},{20,16},{24,20},{28,24},{1,29},{... | collective-permute-start | bytes 6291464 | tf_op jit(solution)/shard_map/ppermute | solution.py:29
  597.5 280.4 %all-to-all-start.2 = ((bf16[4,2,917504]{2,1,0:T(2,128)(2,1)}), bf16[4,2,917504]{2,1,0:T(2,128)(2,1)}, u32[]{:S(2)}, u32[]{:S(2)}) async-start(bf16[4,2,917504]{2,1,0:T(2,128)(2,1)} %reshape.134), calls=%async_computation.2 | async-start | bytes 29360128 | tf_op jit(solution)/shard_map/all_to_all | solution.py:83
  877.8 327.1 %all-to-all-start.1 = ((f32[1,4096,1792]{2,0,1:T(1,128)}), f32[1,4096,1792]{2,0,1:T(1,128)}, u32[]{:S(2)}, u32[]{:S(2)}) async-start(f32[1,4096,1792]{2,0,1:T(1,128)} %broadcast_in_dim.38), calls=%async_computation.1 | async-start | bytes 58720256 | tf_op jit(solution)/shard_map/all_to_all | solution.py:84
